TPU v7x, 32 devices: a whole 2x2x4 slice. The times are simulated.
32 devices in a mesh: ctx: 8 (over z, x), heads: 4 (over y, core).
Axes of the slice: x: 2, y: 2, z: 4, core: 2. Of those that a mesh axis runs over, the one named last changes fastest.
Arguments:
- activations: bfloat16 [2048, 8192], P('ctx', 'heads'), may hold values from -20 to 20
- w_query: bfloat16 [8192, 4096], P(None, 'heads'), may hold values from -0.0625 to 0.0625
- w_key: bfloat16 [8192, 1024], P(None, 'heads'), may hold values from -0.0625 to 0.0625
- w_value: bfloat16 [8192, 1024], P(None, 'heads'), may hold values from -0.0625 to 0.0625
- doc_lengths: int32 [8], replicated, may hold values from 1 to 1024, 2048 in all
- block_dest: int32 [32], replicated, may hold values from 0 to 7, as said below
- out_grad: bfloat16 [2048, 4096], P('ctx', 'heads'), may hold values from -6 to 6
Outputs:
- attention: bfloat16 [2048, 4096], P('ctx', 'heads')
- input_grad: bfloat16 [2048, 8192], P('ctx', 'heads')
Inputs may be any that keep to these rules, and one draw needn't show every extreme that they name: `block_dest`: loader block b lies on loader shard b // 4. Each loader shard sends its blocks to different context shards, and each context shard receives exactly 4 blocks, from different loader shards.
All inputs are finite; a program needn't handle non-finite values.
Results may differ from a plain program's by a relative error of at most 0.025.
The roundings to bfloat16 on the way count: a program that leaves them out, or rounds other values in their place, can miss the bound.
Values may be sent and summed in bfloat16 or wider, within the bound.
A program may use at most 128 MiB of HBM per device.

v0:
```python
import math
import jax
import jax.numpy as jnp
from jax import lax
from jax.sharding import PartitionSpec as P

HD = 128
QPK = 4
NEG = -1e30


def from_behind(value, axis, steps):
    count = lax.axis_size(axis)
    pairs = [(source, (source + steps) % count) for source in range(count)]
    return lax.ppermute(value, axis, pairs)


def layout(block_dest, block_rows):
    nblk = block_dest.shape[0]
    index = jnp.arange(nblk, dtype=jnp.int32)
    order_key = block_dest * nblk + index
    ranks = jnp.sum((order_key[None, :] < order_key[:, None]).astype(jnp.int32), axis=1)
    ctx_blocks = jnp.sum(jnp.where(ranks[None, :] == index[:, None], index[None, :], 0), axis=1)
    ctx_pos = (
        ctx_blocks[:, None] * block_rows + jnp.arange(block_rows, dtype=jnp.int32)[None, :]
    ).reshape(-1)
    return (ctx_blocks, ctx_pos)


def doc_ids(positions, doc_lengths):
    ends = jnp.cumsum(doc_lengths)
    return jnp.sum((ends[None, :] <= positions[:, None]).astype(jnp.int32), axis=1)


def spread(table, array, block_rows):
    width = array.shape[-1]
    grouped = array.reshape(table.shape[1], block_rows, width)
    moved = jnp.einsum("ab,brf->arf", table, grouped, preferred_element_type=jnp.float32)
    return moved.astype(jnp.bfloat16)


def transposed_dot(left, weight):
    return lax.dot_general(
        left, weight, (((1,), (1,)), ((), ())), preferred_element_type=jnp.float32
    )


def per_device(activations, w_query, w_key, w_value, doc_lengths, block_dest, out_grad):
    ctx_count = lax.axis_size("ctx")
    ctx_rank = lax.axis_index("ctx")
    tok_dev = activations.shape[0]
    block_rows = tok_dev * ctx_count // block_dest.shape[0]
    blocks_here = tok_dev // block_rows
    head_dim = HD
    groups = w_key.shape[1] // head_dim
    per_group = QPK
    scale = 1.0 / math.sqrt(head_dim)
    ctx_blocks, ctx_pos = layout(block_dest, block_rows)
    ctx_doc = doc_ids(ctx_pos, doc_lengths)
    my_pos = lax.dynamic_slice_in_dim(ctx_pos, ctx_rank * tok_dev, tok_dev, 0)
    my_doc = lax.dynamic_slice_in_dim(ctx_doc, ctx_rank * tok_dev, tok_dev, 0)
    piece = lax.all_gather(activations, "heads", axis=1, tiled=True)
    rows = piece.shape[1]
    proj_q = jnp.dot(piece, w_query, preferred_element_type=jnp.float32)
    proj_k = jnp.dot(piece, w_key, preferred_element_type=jnp.float32)
    proj_v = jnp.dot(piece, w_value, preferred_element_type=jnp.float32)
    loader_q = proj_q.astype(jnp.bfloat16)
    loader_k = proj_k.astype(jnp.bfloat16)
    loader_v = proj_v.astype(jnp.bfloat16)
    slots = jnp.arange(ctx_count, dtype=jnp.int32)
    my_dest = lax.dynamic_slice_in_dim(block_dest, ctx_rank * blocks_here, blocks_here, 0)
    send_map = (my_dest[None, :] == slots[:, None]).astype(jnp.bfloat16)
    mine = lax.dynamic_slice_in_dim(ctx_blocks, ctx_rank * blocks_here, blocks_here, 0)
    source = mine // blocks_here
    take_map = (source[:, None] == slots[None, :]).astype(jnp.bfloat16)
    recv_q, recv_k, recv_v = (
        lax.all_to_all(
            spread(send_map, loader_q, block_rows), "ctx", split_axis=0, concat_axis=0, tiled=True
        ),
        lax.all_to_all(
            spread(send_map, loader_k, block_rows), "ctx", split_axis=0, concat_axis=0, tiled=True
        ),
        lax.all_to_all(
            spread(send_map, loader_v, block_rows), "ctx", split_axis=0, concat_axis=0, tiled=True
        ),
    )
    ctx_q = spread(take_map, recv_q.reshape(ctx_count * block_rows, -1), block_rows).reshape(
        tok_dev, -1
    )
    ctx_k = spread(take_map, recv_k.reshape(ctx_count * block_rows, -1), block_rows).reshape(
        tok_dev, -1
    )
    ctx_v = spread(take_map, recv_v.reshape(ctx_count * block_rows, -1), block_rows).reshape(
        tok_dev, -1
    )
    query_four = ctx_q.reshape(tok_dev, groups, per_group, head_dim)

    def visible(key_pos, key_doc):
        return (my_doc[:, None] == key_doc[None, :]) & (key_pos[None, :] <= my_pos[:, None])

    def attend(state, key_blk, value_blk, key_pos, key_doc):
        mask = visible(key_pos, key_doc)

        def attend_run(inner):
            m_old, l_old, accum = inner
            scores = (
                jnp.einsum(
                    "tgqe,sge->gqts", query_four, key_blk, preferred_element_type=jnp.float32
                )
                * scale
            )
            scores = jnp.where(mask[None, None], scores, NEG)
            m_new = jnp.maximum(m_old, jnp.max(scores, axis=-1))
            factor = jnp.exp(m_old - m_new)
            probs = jnp.where(mask[None, None], jnp.exp(scores - m_new[..., None]), 0.0)
            l_new = l_old * factor + jnp.sum(probs, axis=-1)
            accum = accum * factor[..., None] + jnp.einsum(
                "gqts,sge->gqte",
                probs,
                value_blk.astype(jnp.float32),
                precision=lax.Precision.HIGHEST,
                preferred_element_type=jnp.float32,
            )
            return (m_new, l_new, accum)

        return lax.cond(jnp.any(mask), attend_run, lambda inner: inner, state)

    start_state = (
        jnp.full((groups, per_group, tok_dev), NEG, jnp.float32),
        jnp.zeros((groups, per_group, tok_dev), jnp.float32),
        jnp.zeros((groups, per_group, tok_dev, head_dim), jnp.float32),
    )
    grad_four = out_grad.reshape(tok_dev, groups, per_group, head_dim)

    def grads_over(dquery, key_piece, value_piece, start, lse, delta):
        rows = key_piece.shape[0]
        width = math.gcd(rows, 512)

        def grads_one_block(index, inner):
            dq_sum, dk_rows, dv_rows = inner
            offset = index * width
            key_blk = key_piece.reshape(width, groups, head_dim)
            value_blk = value_piece.reshape(width, groups, head_dim)
            key_pos = lax.dynamic_slice_in_dim(ctx_pos, start + offset, width, 0)
            key_doc = lax.dynamic_slice_in_dim(ctx_doc, start + offset, width, 0)
            mask = visible(key_pos, key_doc)

            def one_run(unused):
                scores = (
                    jnp.einsum(
                        "tgqe,sge->gqts", query_four, key_blk, preferred_element_type=jnp.float32
                    )
                    * scale
                )
                weights = jnp.where(mask[None, None], jnp.exp(scores - lse[..., None]), 0.0)
                weights_b = weights.astype(jnp.bfloat16)
                dv_blk = jnp.einsum(
                    "gqts,tgqe->sge", weights_b, grad_four, preferred_element_type=jnp.float32
                )
                dprob = jnp.einsum(
                    "tgqe,sge->gqts", grad_four, value_blk, preferred_element_type=jnp.float32
                )
                dscore = (weights * (dprob - delta[..., None]) * scale).astype(jnp.bfloat16)
                dq_add = jnp.einsum(
                    "gqts,sge->tgqe", dscore, key_blk, preferred_element_type=jnp.float32
                )
                dk_blk = jnp.einsum(
                    "gqts,tgqe->sge", dscore, query_four, preferred_element_type=jnp.float32
                )
                return (dq_add, dk_blk, dv_blk)

            def skip(unused):
                return (
                    jnp.zeros((tok_dev, groups, per_group, head_dim), jnp.float32),
                    jnp.zeros((width, groups, head_dim), jnp.float32),
                    jnp.zeros((width, groups, head_dim), jnp.float32),
                )

            dq_add, dk_blk, dv_blk = lax.cond(jnp.any(mask), one_run, skip, 0)
            dk_rows = dk_blk.reshape(width, groups * head_dim)
            dv_rows = dv_blk.reshape(width, groups * head_dim)
            return (dq_sum + dq_add, dk_rows, dv_rows)

        empty_rows = jnp.zeros((rows, groups * head_dim), jnp.float32)
        return lax.fori_loop(0, rows // width, grads_one_block, (dquery, empty_rows, empty_rows))

    dq_start = jnp.zeros((tok_dev, groups, per_group, head_dim), jnp.float32)
    key_piece = lax.all_gather(ctx_k, "ctx", axis=0, tiled=True)
    value_piece = lax.all_gather(ctx_v, "ctx", axis=0, tiled=True)
    rows = key_piece.shape[0]
    width = math.gcd(rows, 512)

    def fold_one_block(index, inner):
        offset = index * width
        key_blk = lax.dynamic_slice_in_dim(key_piece, offset, width, 0).reshape(
            width, groups, head_dim
        )
        value_blk = lax.dynamic_slice_in_dim(value_piece, offset, width, 0).reshape(
            width, groups, head_dim
        )
        key_pos = lax.dynamic_slice_in_dim(ctx_pos, offset, width, 0)
        key_doc = lax.dynamic_slice_in_dim(ctx_doc, offset, width, 0)
        return attend(inner, key_blk, value_blk, key_pos, key_doc)

    m_end, l_end, accum = lax.fori_loop(0, rows // width, fold_one_block, start_state)
    attn = (accum / l_end[..., None]).astype(jnp.bfloat16)
    attention = attn.transpose(2, 0, 1, 3).reshape(tok_dev, groups * per_group * head_dim)
    lse = m_end + jnp.log(l_end)
    attn_four = attention.reshape(tok_dev, groups, per_group, head_dim)
    delta = jnp.einsum(
        "tgqe,tgqe->gqt", grad_four.astype(jnp.float32), attn_four.astype(jnp.float32)
    )

    def turn(step, inner):
        dquery, key_now, value_now, dk_now, dv_now = inner
        owner = jnp.mod(ctx_rank - step, ctx_count)
        dquery, dk_add, dv_add = grads_over(dquery, key_now, value_now, owner * tok_dev, lse, delta)
        dk_now, dv_now = (
            from_behind((dk_now + dk_add).astype(jnp.bfloat16), "ctx", 1).astype(jnp.float32),
            from_behind((dv_now + dv_add).astype(jnp.bfloat16), "ctx", 1).astype(jnp.float32),
        )
        key_now, value_now = from_behind((key_now, value_now), "ctx", 1)
        return (dquery, key_now, value_now, dk_now, dv_now)

    zero_grads = jnp.zeros((tok_dev, groups * head_dim), jnp.float32)
    dquery, unused_k, unused_v, dkey, dvalue = lax.fori_loop(
        0, ctx_count, turn, (dq_start, ctx_k, ctx_v, zero_grads, zero_grads)
    )
    dq_ctx = dquery.reshape(tok_dev, groups * per_group * head_dim).astype(jnp.bfloat16)
    dk_ctx = dkey.astype(jnp.bfloat16)
    dv_ctx = dvalue.astype(jnp.bfloat16)
    back_map = take_map.T
    home_q, home_k, home_v = (
        lax.all_to_all(
            spread(back_map, dq_ctx, block_rows), "ctx", split_axis=0, concat_axis=0, tiled=True
        ),
        lax.all_to_all(
            spread(back_map, dk_ctx, block_rows), "ctx", split_axis=0, concat_axis=0, tiled=True
        ),
        lax.all_to_all(
            spread(back_map, dv_ctx, block_rows), "ctx", split_axis=0, concat_axis=0, tiled=True
        ),
    )
    pick_map = send_map.T
    dq_loader = spread(pick_map, home_q.reshape(ctx_count * block_rows, -1), block_rows).reshape(
        tok_dev, -1
    )
    dk_loader = spread(pick_map, home_k.reshape(ctx_count * block_rows, -1), block_rows).reshape(
        tok_dev, -1
    )
    dv_loader = spread(pick_map, home_v.reshape(ctx_count * block_rows, -1), block_rows).reshape(
        tok_dev, -1
    )
    grad_terms = (
        transposed_dot(dq_loader, w_query)
        + transposed_dot(dk_loader, w_key)
        + transposed_dot(dv_loader, w_value)
    )
    input_grad = lax.psum_scatter(
        grad_terms.astype(jnp.bfloat16), "heads", scatter_dimension=1, tiled=True
    )
    return (attention, input_grad)


def solution(mesh):
    return jax.shard_map(
        per_device,
        mesh=mesh,
        in_specs=(
            P("ctx", "heads"),
            P(None, "heads"),
            P(None, "heads"),
            P(None, "heads"),
            P(),
            P(),
            P("ctx", "heads"),
        ),
        out_specs=(P("ctx", "heads"), P("ctx", "heads")),
        check_vma=False,
    )
```

profile of v0, /device:TPU:0, one launch (start us, length us, event | category | flops | bytes accessed | tf_op | source)
XLA Modules:
  0.0 553.3 jit_solution(3324979120740839685)
XLA Ops:
  9.7 37.1 %all-gather.4.cloned.1.call-done = bf16[256,8192]{1,0:T(8,128)(2,1)} async-done(((bf16[256,2048]{1,0:T(8,128)(2,1)}), bf16[256,8192]{1,0:T(8,128)(2,1)}) %all-gather.4.cloned.1.call-update) | async-done | bytes 4194320 | tf_op jit(solution)/shard_map/all_gather | solution.py:62
  46.8 4.7 convolution_convert_fusion.13
  52.6 5.5 all-to-all-start.2
  58.1 4.7 convolution_convert_fusion.14
  72.1 11.5 %convolution_convert_fusion.4 = bf16[256,1024]{1,0:T(8,128)(2,1)S(1)} fusion(bf16[256,8192]{1,0:T(8,128)(2,1)} %all-gather.4.cloned.1.call-done, bf16[8192,1024]{1,0:T(8,128)(2,1)} %param.16), kind=kOutput, calls=%fused_computation.45 | convolution fusion | flops 4295229440 | bytes 21495808 | tf_op jit(solution)/shard_map/dot_general | solution.py:64
  85.8 6.0 %all-to-all-start.1 = ((bf16[8,64,1024]{2,1,0:T(8,128)(2,1)}), bf16[8,64,1024]{2,1,0:T(8,128)(2,1)S(1)}, u32[]{:S(2)}, u32[]{:S(2)}) async-start(bf16[8,64,1024]{2,1,0:T(8,128)(2,1)} %copy.107), calls=%async_computation.1 | async-start | bytes 2097152 | tf_op jit(solution)/shard_map/all_to_all | solution.py:77
  98.1 27.5 %all-to-all-done.1 = bf16[8,64,1024]{2,1,0:T(8,128)(2,1)S(1)} async-done(((bf16[8,64,1024]{2,1,0:T(8,128)(2,1)}), bf16[8,64,1024]{2,1,0:T(8,128)(2,1)S(1)}, u32[]{:S(2)}, u32[]{:S(2)}) %all-to-all-start.1) | async-done | bytes 1048608 | tf_op jit(solution)/shard_map/all_to_all | solution.py:77
  129.8 36.9 %all-gather.6.cloned.1.call-done = bf16[2048,256]{1,0:T(8,128)(2,1)} async-done(((bf16[256,256]{1,0:T(8,128)(2,1)}), bf16[2048,256]{1,0:T(8,128)(2,1)}) %all-gather.6.cloned.1.call-update) | async-done | bytes 1048592 | tf_op jit(solution)/shard_map/all_gather | solution.py:188
  170.0 47.4 %while.56 = (s32[]{:T(128)}, f32[2,4,256]{2,1,0:T(4,128)S(1)}, f32[2,4,256]{2,1,0:T(4,128)S(1)}, f32[2,4,256,128]{3,2,1,0:T(8,128)}, s32[256]{0:T(256)}, /*index...) while((s32[]{:T(128)}, f32[2,4,256]{2,1,0:T(4,128)S(1)}, ...), condition=%wide.region_10.11_spmd, body=%wide.region_4.10_spmd.sunk | while | flops 1892683776 | bytes 25835900 | solution.py:205
  173.7 8.2 %conditional.5 = ((f32[2,4,256]{2,1,0:T(4,128)S(1)}, f32[2,4,256]{2,1,0:T(4,128)S(1)}, f32[2,4,256,128]{3,2,1,0:T(8,128)})) conditional(s32[]{:T(128)} %convert_element_type.201, (f32[2,4,256]{2,1,0:T(4,128)S(1)}, f32[2,4,256]{2,1,0:T(4,128)S(1)}, f32[2,4,256,128]{3,2,1,0:T(8,128)}) %tuple.116, (pred[256,512]{0,1:T(8,128)(4,1)S(1)}, ...), branch_computations={%region_6.6_spmd, %region_7.9_spmd} | conditional | flops 1892159488 | bytes 25690204 | solution.py:126
  176.6 4.2 fusion.8
  185.5 8.2 %conditional.5 = ((f32[2,4,256]{2,1,0:T(4,128)S(1)}, f32[2,4,256]{2,1,0:T(4,128)S(1)}, f32[2,4,256,128]{3,2,1,0:T(8,128)})) conditional(s32[]{:T(128)} %convert_element_type.201, (f32[2,4,256]{2,1,0:T(4,128)S(1)}, f32[2,4,256]{2,1,0:T(4,128)S(1)}, f32[2,4,256,128]{3,2,1,0:T(8,128)}) %tuple.116, (pred[256,512]{0,1:T(8,128)(4,1)S(1)}, ...), branch_computations={%region_6.6_spmd, %region_7.9_spmd} | conditional | flops 1892159488 | bytes 25690204 | solution.py:126
  197.4 8.2 %conditional.5 = ((f32[2,4,256]{2,1,0:T(4,128)S(1)}, f32[2,4,256]{2,1,0:T(4,128)S(1)}, f32[2,4,256,128]{3,2,1,0:T(8,128)})) conditional(s32[]{:T(128)} %convert_element_type.201, (f32[2,4,256]{2,1,0:T(4,128)S(1)}, f32[2,4,256]{2,1,0:T(4,128)S(1)}, f32[2,4,256,128]{3,2,1,0:T(8,128)}) %tuple.116, (pred[256,512]{0,1:T(8,128)(4,1)S(1)}, ...), branch_computations={%region_6.6_spmd, %region_7.9_spmd} | conditional | flops 1892159488 | bytes 25690204 | solution.py:126
  209.2 8.2 %conditional.5 = ((f32[2,4,256]{2,1,0:T(4,128)S(1)}, f32[2,4,256]{2,1,0:T(4,128)S(1)}, f32[2,4,256,128]{3,2,1,0:T(8,128)})) conditional(s32[]{:T(128)} %convert_element_type.201, (f32[2,4,256]{2,1,0:T(4,128)S(1)}, f32[2,4,256]{2,1,0:T(4,128)S(1)}, f32[2,4,256,128]{3,2,1,0:T(8,128)}) %tuple.116, (pred[256,512]{0,1:T(8,128)(4,1)S(1)}, ...), branch_computations={%region_6.6_spmd, %region_7.9_spmd} | conditional | flops 1892159488 | bytes 25690204 | solution.py:126
  222.4 202.9 %while.57 = (s32[]{:T(128)}, f32[256,2,4,128]{3,0,2,1:T(8,128)S(1)}, bf16[256,256]{1,0:T(8,128)(2,1)}, bf16[256,256]{1,0:T(8,128)(2,1)}, f32[256,256]{0,1:T(8,12...) while((s32[]{:T(128)}, ...), condition=%wide.region_15.16_spmd.clone, body=%wide.region_11.15_spmd.clone.sunk | while | flops 676593664 | bytes 24142468 | solution.py:226
  231.7 5.6 %conditional.6 = (f32[256,2,4,128]{3,0,2,1:T(8,128)S(1)}, f32[256,256]{0,1:T(8,128)S(1)}, f32[256,256]{0,1:T(8,128)S(1)}) conditional(s32[]{:T(128)} %convert_element_type.204, () %tuple.120, (pred[256,256]{0,1:T(8,128)(4,1)}, bf16[256,256]{1,0:T(8,128)(2,1)}, bf16[256,2,4,128]{0,3,2,1:T(8,128)(2,1)}, f32[2,4,256]{2,1,0:T(4,128)}, ...), branch_computations={%region_13.13_spmd, %region_14.14_spmd} | conditional | flops 675282944 | bytes 16203828 | solution.py:179
  240.0 5.5 collective-permute-done.3
  255.6 5.6 %conditional.6 = (f32[256,2,4,128]{3,0,2,1:T(8,128)S(1)}, f32[256,256]{0,1:T(8,128)S(1)}, f32[256,256]{0,1:T(8,128)S(1)}) conditional(s32[]{:T(128)} %convert_element_type.204, () %tuple.120, (pred[256,256]{0,1:T(8,128)(4,1)}, bf16[256,256]{1,0:T(8,128)(2,1)}, bf16[256,2,4,128]{0,3,2,1:T(8,128)(2,1)}, f32[2,4,256]{2,1,0:T(4,128)}, ...), branch_computations={%region_13.13_spmd, %region_14.14_spmd} | conditional | flops 675282944 | bytes 16203828 | solution.py:179
  279.9 5.6 %conditional.6 = (f32[256,2,4,128]{3,0,2,1:T(8,128)S(1)}, f32[256,256]{0,1:T(8,128)S(1)}, f32[256,256]{0,1:T(8,128)S(1)}) conditional(s32[]{:T(128)} %convert_element_type.204, () %tuple.120, (pred[256,256]{0,1:T(8,128)(4,1)}, bf16[256,256]{1,0:T(8,128)(2,1)}, bf16[256,2,4,128]{0,3,2,1:T(8,128)(2,1)}, f32[2,4,256]{2,1,0:T(4,128)}, ...), branch_computations={%region_13.13_spmd, %region_14.14_spmd} | conditional | flops 675282944 | bytes 16203828 | solution.py:179
  304.1 5.6 %conditional.6 = (f32[256,2,4,128]{3,0,2,1:T(8,128)S(1)}, f32[256,256]{0,1:T(8,128)S(1)}, f32[256,256]{0,1:T(8,128)S(1)}) conditional(s32[]{:T(128)} %convert_element_type.204, () %tuple.120, (pred[256,256]{0,1:T(8,128)(4,1)}, bf16[256,256]{1,0:T(8,128)(2,1)}, bf16[256,2,4,128]{0,3,2,1:T(8,128)(2,1)}, f32[2,4,256]{2,1,0:T(4,128)}, ...), branch_computations={%region_13.13_spmd, %region_14.14_spmd} | conditional | flops 675282944 | bytes 16203828 | solution.py:179
  331.5 5.6 %conditional.6 = (f32[256,2,4,128]{3,0,2,1:T(8,128)S(1)}, f32[256,256]{0,1:T(8,128)S(1)}, f32[256,256]{0,1:T(8,128)S(1)}) conditional(s32[]{:T(128)} %convert_element_type.204, () %tuple.120, (pred[256,256]{0,1:T(8,128)(4,1)}, bf16[256,256]{1,0:T(8,128)(2,1)}, bf16[256,2,4,128]{0,3,2,1:T(8,128)(2,1)}, f32[2,4,256]{2,1,0:T(4,128)}, ...), branch_computations={%region_13.13_spmd, %region_14.14_spmd} | conditional | flops 675282944 | bytes 16203828 | solution.py:179
  339.2 7.0 %collective-permute-done.3 = bf16[256,256]{0,1:T(8,128)(2,1)S(1)} collective-permute-done((bf16[256,256]{0,1:T(8,128)(2,1)S(1)}, bf16[256,256]{0,1:T(8,128)(2,1)S(1)}, u32[]{:S(2)}, u32[]{:S(2)}) %collective-permute-start.3) | collective-permute-done | bytes 131104 | tf_op jit(solution)/shard_map/while/body/eval_jaxpr/ppermute | solution.py:15
  357.0 5.6 %conditional.6 = (f32[256,2,4,128]{3,0,2,1:T(8,128)S(1)}, f32[256,256]{0,1:T(8,128)S(1)}, f32[256,256]{0,1:T(8,128)S(1)}) conditional(s32[]{:T(128)} %convert_element_type.204, () %tuple.120, (pred[256,256]{0,1:T(8,128)(4,1)}, bf16[256,256]{1,0:T(8,128)(2,1)}, bf16[256,2,4,128]{0,3,2,1:T(8,128)(2,1)}, f32[2,4,256]{2,1,0:T(4,128)}, ...), branch_computations={%region_13.13_spmd, %region_14.14_spmd} | conditional | flops 675282944 | bytes 16203828 | solution.py:179
  381.7 5.6 %conditional.6 = (f32[256,2,4,128]{3,0,2,1:T(8,128)S(1)}, f32[256,256]{0,1:T(8,128)S(1)}, f32[256,256]{0,1:T(8,128)S(1)}) conditional(s32[]{:T(128)} %convert_element_type.204, () %tuple.120, (pred[256,256]{0,1:T(8,128)(4,1)}, bf16[256,256]{1,0:T(8,128)(2,1)}, bf16[256,2,4,128]{0,3,2,1:T(8,128)(2,1)}, f32[2,4,256]{2,1,0:T(4,128)}, ...), branch_computations={%region_13.13_spmd, %region_14.14_spmd} | conditional | flops 675282944 | bytes 16203828 | solution.py:179
  408.2 5.6 %conditional.6 = (f32[256,2,4,128]{3,0,2,1:T(8,128)S(1)}, f32[256,256]{0,1:T(8,128)S(1)}, f32[256,256]{0,1:T(8,128)S(1)}) conditional(s32[]{:T(128)} %convert_element_type.204, () %tuple.120, (pred[256,256]{0,1:T(8,128)(4,1)}, bf16[256,256]{1,0:T(8,128)(2,1)}, bf16[256,2,4,128]{0,3,2,1:T(8,128)(2,1)}, f32[2,4,256]{2,1,0:T(4,128)}, ...), branch_computations={%region_13.13_spmd, %region_14.14_spmd} | conditional | flops 675282944 | bytes 16203828 | solution.py:179
  416.9 6.0 %collective-permute-done.3 = bf16[256,256]{0,1:T(8,128)(2,1)S(1)} collective-permute-done((bf16[256,256]{0,1:T(8,128)(2,1)S(1)}, bf16[256,256]{0,1:T(8,128)(2,1)S(1)}, u32[]{:S(2)}, u32[]{:S(2)}) %collective-permute-start.3) | collective-permute-done | bytes 131104 | tf_op jit(solution)/shard_map/while/body/eval_jaxpr/ppermute | solution.py:15
  432.1 6.0 %all-to-all-done.5 = bf16[8,64,256]{2,1,0:T(8,128)(2,1)S(1)} async-done(((bf16[8,64,256]{2,1,0:T(8,128)(2,1)}), bf16[8,64,256]{2,1,0:T(8,128)(2,1)S(1)}, u32[]{:S(2)}, u32[]{:S(2)}) %all-to-all-start.5) | async-done | bytes 262176 | tf_op jit(solution)/shard_map/all_to_all | solution.py:240
  444.8 9.6 %all-to-all-done.4 = bf16[8,64,256]{2,1,0:T(8,128)(2,1)S(1)} async-done(((bf16[8,64,256]{2,1,0:T(8,128)(2,1)}), bf16[8,64,256]{2,1,0:T(8,128)(2,1)S(1)}, u32[]{:S(2)}, u32[]{:S(2)}) %all-to-all-start.4) | async-done | bytes 262176 | tf_op jit(solution)/shard_map/all_to_all | solution.py:237
  458.7 15.6 %all-to-all-done.3 = bf16[8,64,1024]{2,1,0:T(8,128)(2,1)S(1)} async-done(((bf16[8,64,1024]{2,1,0:T(8,128)(2,1)}), bf16[8,64,1024]{2,1,0:T(8,128)(2,1)S(1)}, u32[]{:S(2)}, u32[]{:S(2)}) %all-to-all-start.3) | async-done | bytes 1048608 | tf_op jit(solution)/shard_map/all_to_all | solution.py:234
  475.3 18.9 %fusion.56 = f32[256,8192]{1,0:T(8,128)} fusion(bf16[256,1024]{1,0:T(8,128)(2,1)S(1)} %bitcast.128, bf16[8192,1024]{1,0:T(8,128)(2,1)} %param.16), kind=kOutput, calls=%fused_computation.91 | convolution fusion | flops 4294967296 | bytes 25690112 | tf_op jit(solution)/shard_map/dot_general | solution.py:43
  494.2 6.1 %convolution_add_fusion.1 = f32[256,8192]{1,0:T(8,128)S(1)} fusion(f32[256,8192]{1,0:T(8,128)} %fusion.56, bf16[256,256]{1,0:T(8,128)(2,1)S(1)} %bitcast.133, bf16[8192,256]{1,0:T(8,128)(2,1)} %param.17), kind=kOutput, calls=%fused_computation.39 | convolution fusion | flops 1075838976 | bytes 21102592 | tf_op jit(solution)/shard_map/dot_general | solution.py:43
  506.2 40.6 %reduce-scatter.2.cloned.1.call-done = bf16[256,2048]{1,0:T(8,128)(2,1)} async-done(((bf16[256,8192]{1,0:T(8,128)(2,1)}), bf16[256,2048]{1,0:T(8,128)(2,1)}) %reduce-scatter.2.cloned.1.call-update) | async-done | bytes 1048592 | tf_op jit(solution)/shard_map/reduce_scatter | solution.py:259
  (359 shorter events, 277.6 us)
Async XLA Ops:
  7.2 39.6 %all-gather.4.cloned.1.call-start = ((), (), s32[]{:S(2)}) async-start(), calls=%async_computation.7 | async-start | bytes 5242880 | tf_op jit(solution)/shard_map/all_gather | solution.py:62
  52.6 14.8 %all-to-all-start.2 = ((bf16[8,64,256]{2,1,0:T(8,128)(2,1)}), bf16[8,64,256]{2,1,0:T(8,128)(2,1)S(1)}, u32[]{:S(2)}, u32[]{:S(2)}) async-start(bf16[8,64,256]{2,1,0:T(8,128)(2,1)} %copy.111), calls=%async_computation.2 | async-start | bytes 524288 | tf_op jit(solution)/shard_map/all_to_all | solution.py:83
  67.4 18.4 %all-to-all-start = ((bf16[8,64,256]{2,1,0:T(8,128)(2,1)}), bf16[8,64,256]{2,1,0:T(8,128)(2,1)S(1)}, u32[]{:S(2)}, u32[]{:S(2)}) async-start(bf16[8,64,256]{2,1,0:T(8,128)(2,1)} %copy.103), calls=%async_computation | async-start | bytes 524288 | tf_op jit(solution)/shard_map/all_to_all | solution.py:80
  71.0 57.1 %all-gather.8.cloned.1.call-start = ((), (), s32[]{:S(2)}) async-start(), calls=%async_computation.9 | async-start | bytes 1179648 | tf_op jit(solution)/shard_map/all_gather | solution.py:189
  85.8 39.7 %all-to-all-start.1 = ((bf16[8,64,1024]{2,1,0:T(8,128)(2,1)}), bf16[8,64,1024]{2,1,0:T(8,128)(2,1)S(1)}, u32[]{:S(2)}, u32[]{:S(2)}) async-start(bf16[8,64,1024]{2,1,0:T(8,128)(2,1)} %copy.107), calls=%async_computation.1 | async-start | bytes 2097152 | tf_op jit(solution)/shard_map/all_to_all | solution.py:77
  91.8 74.8 %all-gather.6.cloned.1.call-start = ((), (), s32[]{:S(2)}) async-start(), calls=%async_computation.8 | async-start | bytes 1179648 | tf_op jit(solution)/shard_map/all_gather | solution.py:188
  224.0 23.6 %collective-permute-start = (bf16[256,256]{1,0:T(8,128)(2,1)}, bf16[256,256]{1,0:T(8,128)(2,1)}, u32[]{:S(2)}, u32[]{:S(2)}) collective-permute-start(bf16[256,256]{1,0:T(8,128)(2,1)} %copy.227), channel_id=1, source_target_pairs={{0,4},{4,8},{8,12},{12,16},{16,20},{20,24},{24,28},{28,0},{1,5},{5... | collective-permute-start | bytes 393224 | tf_op jit(solution)/shard_map/while/body/eval_jaxpr/ppermute | solution.py:15
  226.1 21.5 %collective-permute-start.1 = (bf16[256,256]{1,0:T(8,128)(2,1)}, bf16[256,256]{1,0:T(8,128)(2,1)}, u32[]{:S(2)}, u32[]{:S(2)}) collective-permute-start(bf16[256,256]{1,0:T(8,128)(2,1)} %copy.228), channel_id=1, source_target_pairs={{0,4},{4,8},{8,12},{12,16},{16,20},{20,24},{24,28},{28,0},{1,5},{5... | collective-permute-start | bytes 393224 | tf_op jit(solution)/shard_map/while/body/eval_jaxpr/ppermute | solution.py:15
  238.0 8.9 %collective-permute-start.2 = (bf16[256,256]{0,1:T(8,128)(2,1)S(1)}, bf16[256,256]{0,1:T(8,128)(2,1)S(1)}, u32[]{:S(2)}, u32[]{:S(2)}) collective-permute-start(bf16[256,256]{0,1:T(8,128)(2,1)S(1)} %fusion.84), channel_id=1, source_target_pairs={{0,4},{4,8},{8,12},{12,16},{16,20},{20,24},{24,28},{28,0},{1,5},{5... | collective-permute-start | bytes 393224 | tf_op jit(solution)/shard_map/while/body/eval_jaxpr/ppermute | solution.py:15
  249.2 22.0 %collective-permute-start = (bf16[256,256]{1,0:T(8,128)(2,1)}, bf16[256,256]{1,0:T(8,128)(2,1)}, u32[]{:S(2)}, u32[]{:S(2)}) collective-permute-start(bf16[256,256]{1,0:T(8,128)(2,1)} %copy.227), channel_id=1, source_target_pairs={{0,4},{4,8},{8,12},{12,16},{16,20},{20,24},{24,28},{28,0},{1,5},{5... | collective-permute-start | bytes 393224 | tf_op jit(solution)/shard_map/while/body/eval_jaxpr/ppermute | solution.py:15
  250.8 20.4 %collective-permute-start.1 = (bf16[256,256]{1,0:T(8,128)(2,1)}, bf16[256,256]{1,0:T(8,128)(2,1)}, u32[]{:S(2)}, u32[]{:S(2)}) collective-permute-start(bf16[256,256]{1,0:T(8,128)(2,1)} %copy.228), channel_id=1, source_target_pairs={{0,4},{4,8},{8,12},{12,16},{16,20},{20,24},{24,28},{28,0},{1,5},{5... | collective-permute-start | bytes 393224 | tf_op jit(solution)/shard_map/while/body/eval_jaxpr/ppermute | solution.py:15
  272.8 23.7 %collective-permute-start = (bf16[256,256]{1,0:T(8,128)(2,1)}, bf16[256,256]{1,0:T(8,128)(2,1)}, u32[]{:S(2)}, u32[]{:S(2)}) collective-permute-start(bf16[256,256]{1,0:T(8,128)(2,1)} %copy.227), channel_id=1, source_target_pairs={{0,4},{4,8},{8,12},{12,16},{16,20},{20,24},{24,28},{28,0},{1,5},{5... | collective-permute-start | bytes 393224 | tf_op jit(solution)/shard_map/while/body/eval_jaxpr/ppermute | solution.py:15
  274.4 22.1 %collective-permute-start.1 = (bf16[256,256]{1,0:T(8,128)(2,1)}, bf16[256,256]{1,0:T(8,128)(2,1)}, u32[]{:S(2)}, u32[]{:S(2)}) collective-permute-start(bf16[256,256]{1,0:T(8,128)(2,1)} %copy.228), channel_id=1, source_target_pairs={{0,4},{4,8},{8,12},{12,16},{16,20},{20,24},{24,28},{28,0},{1,5},{5... | collective-permute-start | bytes 393224 | tf_op jit(solution)/shard_map/while/body/eval_jaxpr/ppermute | solution.py:15
  298.1 23.9 %collective-permute-start = (bf16[256,256]{1,0:T(8,128)(2,1)}, bf16[256,256]{1,0:T(8,128)(2,1)}, u32[]{:S(2)}, u32[]{:S(2)}) collective-permute-start(bf16[256,256]{1,0:T(8,128)(2,1)} %copy.227), channel_id=1, source_target_pairs={{0,4},{4,8},{8,12},{12,16},{16,20},{20,24},{24,28},{28,0},{1,5},{5... | collective-permute-start | bytes 393224 | tf_op jit(solution)/shard_map/while/body/eval_jaxpr/ppermute | solution.py:15
  299.6 22.3 %collective-permute-start.1 = (bf16[256,256]{1,0:T(8,128)(2,1)}, bf16[256,256]{1,0:T(8,128)(2,1)}, u32[]{:S(2)}, u32[]{:S(2)}) collective-permute-start(bf16[256,256]{1,0:T(8,128)(2,1)} %copy.228), channel_id=1, source_target_pairs={{0,4},{4,8},{8,12},{12,16},{16,20},{20,24},{24,28},{28,0},{1,5},{5... | collective-permute-start | bytes 393224 | tf_op jit(solution)/shard_map/while/body/eval_jaxpr/ppermute | solution.py:15
  323.5 26.3 %collective-permute-start = (bf16[256,256]{1,0:T(8,128)(2,1)}, bf16[256,256]{1,0:T(8,128)(2,1)}, u32[]{:S(2)}, u32[]{:S(2)}) collective-permute-start(bf16[256,256]{1,0:T(8,128)(2,1)} %copy.227), channel_id=1, source_target_pairs={{0,4},{4,8},{8,12},{12,16},{16,20},{20,24},{24,28},{28,0},{1,5},{5... | collective-permute-start | bytes 393224 | tf_op jit(solution)/shard_map/while/body/eval_jaxpr/ppermute | solution.py:15
  325.1 24.7 %collective-permute-start.1 = (bf16[256,256]{1,0:T(8,128)(2,1)}, bf16[256,256]{1,0:T(8,128)(2,1)}, u32[]{:S(2)}, u32[]{:S(2)}) collective-permute-start(bf16[256,256]{1,0:T(8,128)(2,1)} %copy.228), channel_id=1, source_target_pairs={{0,4},{4,8},{8,12},{12,16},{16,20},{20,24},{24,28},{28,0},{1,5},{5... | collective-permute-start | bytes 393224 | tf_op jit(solution)/shard_map/while/body/eval_jaxpr/ppermute | solution.py:15
  337.2 9.1 %collective-permute-start.3 = (bf16[256,256]{0,1:T(8,128)(2,1)S(1)}, bf16[256,256]{0,1:T(8,128)(2,1)S(1)}, u32[]{:S(2)}, u32[]{:S(2)}) collective-permute-start(bf16[256,256]{0,1:T(8,128)(2,1)S(1)} %fusion.85), channel_id=1, source_target_pairs={{0,4},{4,8},{8,12},{12,16},{16,20},{20,24},{24,28},{28,0},{1,5},{5... | collective-permute-start | bytes 393224 | tf_op jit(solution)/shard_map/while/body/eval_jaxpr/ppermute | solution.py:15
  338.8 10.2 %collective-permute-start.2 = (bf16[256,256]{0,1:T(8,128)(2,1)S(1)}, bf16[256,256]{0,1:T(8,128)(2,1)S(1)}, u32[]{:S(2)}, u32[]{:S(2)}) collective-permute-start(bf16[256,256]{0,1:T(8,128)(2,1)S(1)} %fusion.84), channel_id=1, source_target_pairs={{0,4},{4,8},{8,12},{12,16},{16,20},{20,24},{24,28},{28,0},{1,5},{5... | collective-permute-start | bytes 393224 | tf_op jit(solution)/shard_map/while/body/eval_jaxpr/ppermute | solution.py:15
  351.3 21.6 %collective-permute-start = (bf16[256,256]{1,0:T(8,128)(2,1)}, bf16[256,256]{1,0:T(8,128)(2,1)}, u32[]{:S(2)}, u32[]{:S(2)}) collective-permute-start(bf16[256,256]{1,0:T(8,128)(2,1)} %copy.227), channel_id=1, source_target_pairs={{0,4},{4,8},{8,12},{12,16},{16,20},{20,24},{24,28},{28,0},{1,5},{5... | collective-permute-start | bytes 393224 | tf_op jit(solution)/shard_map/while/body/eval_jaxpr/ppermute | solution.py:15
  352.9 20.1 %collective-permute-start.1 = (bf16[256,256]{1,0:T(8,128)(2,1)}, bf16[256,256]{1,0:T(8,128)(2,1)}, u32[]{:S(2)}, u32[]{:S(2)}) collective-permute-start(bf16[256,256]{1,0:T(8,128)(2,1)} %copy.228), channel_id=1, source_target_pairs={{0,4},{4,8},{8,12},{12,16},{16,20},{20,24},{24,28},{28,0},{1,5},{5... | collective-permute-start | bytes 393224 | tf_op jit(solution)/shard_map/while/body/eval_jaxpr/ppermute | solution.py:15
  374.5 24.0 %collective-permute-start = (bf16[256,256]{1,0:T(8,128)(2,1)}, bf16[256,256]{1,0:T(8,128)(2,1)}, u32[]{:S(2)}, u32[]{:S(2)}) collective-permute-start(bf16[256,256]{1,0:T(8,128)(2,1)} %copy.227), channel_id=1, source_target_pairs={{0,4},{4,8},{8,12},{12,16},{16,20},{20,24},{24,28},{28,0},{1,5},{5... | collective-permute-start | bytes 393224 | tf_op jit(solution)/shard_map/while/body/eval_jaxpr/ppermute | solution.py:15
  376.1 22.5 %collective-permute-start.1 = (bf16[256,256]{1,0:T(8,128)(2,1)}, bf16[256,256]{1,0:T(8,128)(2,1)}, u32[]{:S(2)}, u32[]{:S(2)}) collective-permute-start(bf16[256,256]{1,0:T(8,128)(2,1)} %copy.228), channel_id=1, source_target_pairs={{0,4},{4,8},{8,12},{12,16},{16,20},{20,24},{24,28},{28,0},{1,5},{5... | collective-permute-start | bytes 393224 | tf_op jit(solution)/shard_map/while/body/eval_jaxpr/ppermute | solution.py:15
  387.3 9.0 %collective-permute-start.3 = (bf16[256,256]{0,1:T(8,128)(2,1)S(1)}, bf16[256,256]{0,1:T(8,128)(2,1)S(1)}, u32[]{:S(2)}, u32[]{:S(2)}) collective-permute-start(bf16[256,256]{0,1:T(8,128)(2,1)S(1)} %fusion.85), channel_id=1, source_target_pairs={{0,4},{4,8},{8,12},{12,16},{16,20},{20,24},{24,28},{28,0},{1,5},{5... | collective-permute-start | bytes 393224 | tf_op jit(solution)/shard_map/while/body/eval_jaxpr/ppermute | solution.py:15
  400.1 25.2 %collective-permute-start = (bf16[256,256]{1,0:T(8,128)(2,1)}, bf16[256,256]{1,0:T(8,128)(2,1)}, u32[]{:S(2)}, u32[]{:S(2)}) collective-permute-start(bf16[256,256]{1,0:T(8,128)(2,1)} %copy.227), channel_id=1, source_target_pairs={{0,4},{4,8},{8,12},{12,16},{16,20},{20,24},{24,28},{28,0},{1,5},{5... | collective-permute-start | bytes 393224 | tf_op jit(solution)/shard_map/while/body/eval_jaxpr/ppermute | solution.py:15
  401.7 23.6 %collective-permute-start.1 = (bf16[256,256]{1,0:T(8,128)(2,1)}, bf16[256,256]{1,0:T(8,128)(2,1)}, u32[]{:S(2)}, u32[]{:S(2)}) collective-permute-start(bf16[256,256]{1,0:T(8,128)(2,1)} %copy.228), channel_id=1, source_target_pairs={{0,4},{4,8},{8,12},{12,16},{16,20},{20,24},{24,28},{28,0},{1,5},{5... | collective-permute-start | bytes 393224 | tf_op jit(solution)/shard_map/while/body/eval_jaxpr/ppermute | solution.py:15
  413.8 9.0 %collective-permute-start.3 = (bf16[256,256]{0,1:T(8,128)(2,1)S(1)}, bf16[256,256]{0,1:T(8,128)(2,1)S(1)}, u32[]{:S(2)}, u32[]{:S(2)}) collective-permute-start(bf16[256,256]{0,1:T(8,128)(2,1)S(1)} %fusion.85), channel_id=1, source_target_pairs={{0,4},{4,8},{8,12},{12,16},{16,20},{20,24},{24,28},{28,0},{1,5},{5... | collective-permute-start | bytes 393224 | tf_op jit(solution)/shard_map/while/body/eval_jaxpr/ppermute | solution.py:15
  415.2 9.4 %collective-permute-start.2 = (bf16[256,256]{0,1:T(8,128)(2,1)S(1)}, bf16[256,256]{0,1:T(8,128)(2,1)S(1)}, u32[]{:S(2)}, u32[]{:S(2)}) collective-permute-start(bf16[256,256]{0,1:T(8,128)(2,1)S(1)} %fusion.84), channel_id=1, source_target_pairs={{0,4},{4,8},{8,12},{12,16},{16,20},{20,24},{24,28},{28,0},{1,5},{5... | collective-permute-start | bytes 393224 | tf_op jit(solution)/shard_map/while/body/eval_jaxpr/ppermute | solution.py:15
  426.5 11.6 %all-to-all-start.5 = ((bf16[8,64,256]{2,1,0:T(8,128)(2,1)}), bf16[8,64,256]{2,1,0:T(8,128)(2,1)S(1)}, u32[]{:S(2)}, u32[]{:S(2)}) async-start(bf16[8,64,256]{2,1,0:T(8,128)(2,1)} %copy.132), calls=%async_computation.5 | async-start | bytes 524288 | tf_op jit(solution)/shard_map/all_to_all | solution.py:240
  438.1 16.4 %all-to-all-start.4 = ((bf16[8,64,256]{2,1,0:T(8,128)(2,1)}), bf16[8,64,256]{2,1,0:T(8,128)(2,1)S(1)}, u32[]{:S(2)}, u32[]{:S(2)}) async-start(bf16[8,64,256]{2,1,0:T(8,128)(2,1)} %copy.127), calls=%async_computation.4 | async-start | bytes 524288 | tf_op jit(solution)/shard_map/all_to_all | solution.py:237
  454.5 19.9 %all-to-all-start.3 = ((bf16[8,64,1024]{2,1,0:T(8,128)(2,1)}), bf16[8,64,1024]{2,1,0:T(8,128)(2,1)S(1)}, u32[]{:S(2)}, u32[]{:S(2)}) async-start(bf16[8,64,1024]{2,1,0:T(8,128)(2,1)} %copy.122), calls=%async_computation.3 | async-start | bytes 2097152 | tf_op jit(solution)/shard_map/all_to_all | solution.py:234
  458.0 88.7 %reduce-scatter.2.cloned.1.call-start = ((), (), s32[]{:S(2)}) async-start(), calls=%async_computation.10 | async-start | bytes 5242880 | tf_op jit(solution)/shard_map/reduce_scatter | solution.py:259
  (34 other events, 553.7 us)
Sparse Core Ops, SparseCore 0:
  9.6 37.1 all-gather.3
  74.0 51.0 all-gather.7
  127.2 39.3 all-gather.5
  503.7 43.0 reduce-scatter.1
where the time goes:
time: 556 us; the launch traced here: 553 us
  waiting for transfers between devices  231 us (42%)
  matrix products  104 us (19%)
  local copies, waits for them, and re-layouts  90.9 us (16%)
  starting transfers between devices  56.4 us (10%)
  other arithmetic  49 us (9%)
  between operations  14.1 us (3%)
  loops' own time  8.15 us (1%)
    ppermute x32, waiting for transfers between devices, from_behind(): return lax.ppermute(value, axis, pairs)  53.3 us
    reduce_scatter x1, waiting for transfers between devices, per_device(): lax.psum_scatter(grad_terms.astype(jnp.bfloat16), 'heads', scatter_dimens...  40.6 us
    all_gather x1, waiting for transfers between devices, per_device(): piece = lax.all_gather(activations, 'heads', axis=1, tiled=True)  37.1 us
    all_gather x1, waiting for transfers between devices, per_device(): key_piece = lax.all_gather(ctx_k, 'ctx', axis=0, tiled=True)  36.9 us
    ppermute x32, starting transfers between devices, from_behind(): return lax.ppermute(value, axis, pairs)  30.5 us
    dot_general x3, matrix products, transposed_dot(): lax.dot_general(left, weight, (((1,), (1,)), ((), ())), preferred_element...  28.3 us
    all_to_all x1, waiting for transfers between devices, per_device(): lax.all_to_all(spread(send_map, loader_q, block_rows), 'ctx', split_axis=...  27.5 us
    while x16, local copies, waits for them, and re-layouts  25 us
  transfers between devices with their start and end apart: 42, of which 24 were waited for; matrix products, arithmetic and copies ran while one was open for 25% of the time, Pallas kernels for 0%

commit v1 on v0

--- a/solution.py
+++ b/solution.py
@@ -7,6 +7,16 @@
 HD = 128
 QPK = 4
 NEG = -1e30
+
+
+def _resolve_stages_all(block_in, unit):
+    return jnp.split(
+        lax.all_gather(
+            jnp.concatenate([block_in, unit], axis=1), tiled=True, axis=0, axis_name="ctx"
+        ),
+        [block_in.shape[1]],
+        axis=1,
+    )
 
 
 def from_behind(value, axis, steps):
@@ -185,8 +195,7 @@
         return lax.fori_loop(0, rows // width, grads_one_block, (dquery, empty_rows, empty_rows))
 
     dq_start = jnp.zeros((tok_dev, groups, per_group, head_dim), jnp.float32)
-    key_piece = lax.all_gather(ctx_k, "ctx", axis=0, tiled=True)
-    value_piece = lax.all_gather(ctx_v, "ctx", axis=0, tiled=True)
+    key_piece, value_piece = _resolve_stages_all(ctx_k, ctx_v)
     rows = key_piece.shape[0]
     width = math.gcd(rows, 512)
 

time: 556 us -> 539 us (0.969)
  waiting for transfers between devices: 231 us -> 209 us
    all_gather x2 -> x1, waiting for transfers between devices: 36.9 us -> 0.72 us  [_resolve_stages_all(): lax.all_gather(jnp.concatenate([block_in, unit], axis=1), tiled=True, axi...]
    all_to_all x1, waiting for transfers between devices: 0.01 us -> 7.48 us  [per_device(): lax.all_to_all(spread(send_map, loader_k, block_rows), 'ctx', split_axis=...]
    all_to_all x1, waiting for transfers between devices: 27.5 us -> 34.2 us  [per_device(): lax.all_to_all(spread(send_map, loader_q, block_rows), 'ctx', split_axis=...]
  transfers between devices with their start and end apart: 42 -> 41, of which waited for: 24 -> 25; matrix products, arithmetic and copies ran while one was open for 25% -> 26% of each run, Pallas kernels for 0% -> 0%
where the time goes in v1:
time: 539 us; the launch traced here: 536 us
  waiting for transfers between devices  209 us (39%)
  matrix products  104 us (19%)
  local copies, waits for them, and re-layouts  93.3 us (17%)
  starting transfers between devices  55 us (10%)
  other arithmetic  51.3 us (10%)
  between operations  14.1 us (3%)
  loops' own time  9.05 us (2%)
    ppermute x32, waiting for transfers between devices, from_behind(): return lax.ppermute(value, axis, pairs)  52.2 us
    reduce_scatter x1, waiting for transfers between devices, per_device(): lax.psum_scatter(grad_terms.astype(jnp.bfloat16), 'heads', scatter_dimens...  40.6 us
    all_gather x1, waiting for transfers between devices, per_device(): piece = lax.all_gather(activations, 'heads', axis=1, tiled=True)  37.5 us
    all_to_all x1, waiting for transfers between devices, per_device(): lax.all_to_all(spread(send_map, loader_q, block_rows), 'ctx', split_axis=...  34.2 us
    ppermute x32, starting transfers between devices, from_behind(): return lax.ppermute(value, axis, pairs)  30.3 us
    dot_general x3, matrix products, transposed_dot(): lax.dot_general(left, weight, (((1,), (1,)), ((), ())), preferred_element...  28.5 us
    while x16, local copies, waits for them, and re-layouts  25 us
    reduce_or x8, other arithmetic, grads_one_block(): dq_add, dk_blk, dv_blk = lax.cond(jnp.any(mask), one_run, skip, 0)  17 us
  transfers between devices with their start and end apart: 41, of which 25 were waited for; matrix products, arithmetic and copies ran while one was open for 26% of the time, Pallas kernels for 0%

profile of v1, /device:TPU:0, one launch (start us, length us, event | category | flops | bytes accessed | tf_op | source)
XLA Modules:
  0.0 535.7 jit_solution(4103943199858300213)
XLA Ops:
  9.3 37.5 %all-gather.3.cloned.1.call-done = bf16[256,8192]{1,0:T(8,128)(2,1)} async-done(((bf16[256,2048]{1,0:T(8,128)(2,1)}), bf16[256,8192]{1,0:T(8,128)(2,1)}) %all-gather.3.cloned.1.call-update) | async-done | bytes 4194320 | tf_op jit(solution)/shard_map/all_gather | solution.py:72
  46.8 4.7 convolution_convert_fusion.13
  52.6 5.5 %all-to-all-start.1 = ((bf16[8,64,256]{2,1,0:T(8,128)(2,1)}), bf16[8,64,256]{2,1,0:T(8,128)(2,1)S(1)}, u32[]{:S(2)}, u32[]{:S(2)}) async-start(bf16[8,64,256]{2,1,0:T(8,128)(2,1)} %copy.107), calls=%async_computation.1 | async-start | bytes 524288 | tf_op jit(solution)/shard_map/all_to_all | solution.py:93
  58.1 4.7 convolution_convert_fusion.14
  72.4 7.5 %all-to-all-done = bf16[8,64,256]{2,1,0:T(8,128)(2,1)S(1)} async-done(((bf16[8,64,256]{2,1,0:T(8,128)(2,1)}), bf16[8,64,256]{2,1,0:T(8,128)(2,1)S(1)}, u32[]{:S(2)}, u32[]{:S(2)}) %all-to-all-start) | async-done | bytes 262176 | tf_op jit(solution)/shard_map/all_to_all | solution.py:90
  82.6 11.7 %convolution_convert_fusion.4 = bf16[256,1024]{1,0:T(8,128)(2,1)S(1)} fusion(bf16[256,8192]{1,0:T(8,128)(2,1)} %all-gather.3.cloned.1.call-done, bf16[8192,1024]{1,0:T(8,128)(2,1)} %param.16), kind=kOutput, calls=%fused_computation.45 | convolution fusion | flops 4295229440 | bytes 21495808 | tf_op jit(solution)/shard_map/dot_general | solution.py:74
  105.4 34.2 %all-to-all-done.2 = bf16[8,64,1024]{2,1,0:T(8,128)(2,1)S(1)} async-done(((bf16[8,64,1024]{2,1,0:T(8,128)(2,1)}), bf16[8,64,1024]{2,1,0:T(8,128)(2,1)S(1)}, u32[]{:S(2)}, u32[]{:S(2)}) %all-to-all-start.2) | async-done | bytes 1048608 | tf_op jit(solution)/shard_map/all_to_all | solution.py:87
  150.7 47.5 %while.56 = (s32[]{:T(128)}, f32[2,4,256]{2,1,0:T(4,128)S(1)}, f32[2,4,256]{2,1,0:T(4,128)S(1)}, f32[2,4,256,128]{3,2,1,0:T(8,128)}, s32[256]{0:T(256)}, /*index...) while((s32[]{:T(128)}, f32[2,4,256]{2,1,0:T(4,128)S(1)}, ...), condition=%wide.region_10.11_spmd, body=%wide.region_4.10_spmd.sunk | while | flops 1892683776 | bytes 25835900 | solution.py:214
  154.4 8.2 %conditional.5 = ((f32[2,4,256]{2,1,0:T(4,128)S(1)}, f32[2,4,256]{2,1,0:T(4,128)S(1)}, f32[2,4,256,128]{3,2,1,0:T(8,128)})) conditional(s32[]{:T(128)} %convert_element_type.201, (f32[2,4,256]{2,1,0:T(4,128)S(1)}, f32[2,4,256]{2,1,0:T(4,128)S(1)}, f32[2,4,256,128]{3,2,1,0:T(8,128)}) %tuple.117, (pred[256,512]{0,1:T(8,128)(4,1)S(1)}, ...), branch_computations={%region_6.6_spmd, %region_7.9_spmd} | conditional | flops 1892159488 | bytes 25690204 | solution.py:136
  166.3 8.2 %conditional.5 = ((f32[2,4,256]{2,1,0:T(4,128)S(1)}, f32[2,4,256]{2,1,0:T(4,128)S(1)}, f32[2,4,256,128]{3,2,1,0:T(8,128)})) conditional(s32[]{:T(128)} %convert_element_type.201, (f32[2,4,256]{2,1,0:T(4,128)S(1)}, f32[2,4,256]{2,1,0:T(4,128)S(1)}, f32[2,4,256,128]{3,2,1,0:T(8,128)}) %tuple.117, (pred[256,512]{0,1:T(8,128)(4,1)S(1)}, ...), branch_computations={%region_6.6_spmd, %region_7.9_spmd} | conditional | flops 1892159488 | bytes 25690204 | solution.py:136
  178.1 8.2 %conditional.5 = ((f32[2,4,256]{2,1,0:T(4,128)S(1)}, f32[2,4,256]{2,1,0:T(4,128)S(1)}, f32[2,4,256,128]{3,2,1,0:T(8,128)})) conditional(s32[]{:T(128)} %convert_element_type.201, (f32[2,4,256]{2,1,0:T(4,128)S(1)}, f32[2,4,256]{2,1,0:T(4,128)S(1)}, f32[2,4,256,128]{3,2,1,0:T(8,128)}) %tuple.117, (pred[256,512]{0,1:T(8,128)(4,1)S(1)}, ...), branch_computations={%region_6.6_spmd, %region_7.9_spmd} | conditional | flops 1892159488 | bytes 25690204 | solution.py:136
  190.0 8.2 %conditional.5 = ((f32[2,4,256]{2,1,0:T(4,128)S(1)}, f32[2,4,256]{2,1,0:T(4,128)S(1)}, f32[2,4,256,128]{3,2,1,0:T(8,128)})) conditional(s32[]{:T(128)} %convert_element_type.201, (f32[2,4,256]{2,1,0:T(4,128)S(1)}, f32[2,4,256]{2,1,0:T(4,128)S(1)}, f32[2,4,256,128]{3,2,1,0:T(8,128)}) %tuple.117, (pred[256,512]{0,1:T(8,128)(4,1)S(1)}, ...), branch_computations={%region_6.6_spmd, %region_7.9_spmd} | conditional | flops 1892159488 | bytes 25690204 | solution.py:136
  203.2 202.7 %while.57 = (s32[]{:T(128)}, f32[256,2,4,128]{3,0,2,1:T(8,128)S(1)}, bf16[256,256]{1,0:T(8,128)(2,1)}, bf16[256,256]{1,0:T(8,128)(2,1)}, f32[256,256]{0,1:T(8,12...) while((s32[]{:T(128)}, ...), condition=%wide.region_15.16_spmd.clone, body=%wide.region_11.15_spmd.clone.sunk | while | flops 676593664 | bytes 24142468 | solution.py:235
  212.3 5.6 %conditional.6 = (f32[256,2,4,128]{3,0,2,1:T(8,128)S(1)}, f32[256,256]{0,1:T(8,128)S(1)}, f32[256,256]{0,1:T(8,128)S(1)}) conditional(s32[]{:T(128)} %convert_element_type.204, () %tuple.121, (pred[256,256]{0,1:T(8,128)(4,1)}, bf16[256,256]{1,0:T(8,128)(2,1)}, bf16[256,2,4,128]{0,3,2,1:T(8,128)(2,1)}, f32[2,4,256]{2,1,0:T(4,128)}, ...), branch_computations={%region_13.13_spmd, %region_14.14_spmd} | conditional | flops 675282944 | bytes 16203828 | solution.py:189
  221.2 5.9 %collective-permute-done.3 = bf16[256,256]{0,1:T(8,128)(2,1)S(1)} collective-permute-done((bf16[256,256]{0,1:T(8,128)(2,1)S(1)}, bf16[256,256]{0,1:T(8,128)(2,1)S(1)}, u32[]{:S(2)}, u32[]{:S(2)}) %collective-permute-start.3) | collective-permute-done | bytes 131104 | tf_op jit(solution)/shard_map/while/body/eval_jaxpr/ppermute | solution.py:25
  236.9 5.6 %conditional.6 = (f32[256,2,4,128]{3,0,2,1:T(8,128)S(1)}, f32[256,256]{0,1:T(8,128)S(1)}, f32[256,256]{0,1:T(8,128)S(1)}) conditional(s32[]{:T(128)} %convert_element_type.204, () %tuple.121, (pred[256,256]{0,1:T(8,128)(4,1)}, bf16[256,256]{1,0:T(8,128)(2,1)}, bf16[256,2,4,128]{0,3,2,1:T(8,128)(2,1)}, f32[2,4,256]{2,1,0:T(4,128)}, ...), branch_computations={%region_13.13_spmd, %region_14.14_spmd} | conditional | flops 675282944 | bytes 16203828 | solution.py:189
  261.6 5.6 %conditional.6 = (f32[256,2,4,128]{3,0,2,1:T(8,128)S(1)}, f32[256,256]{0,1:T(8,128)S(1)}, f32[256,256]{0,1:T(8,128)S(1)}) conditional(s32[]{:T(128)} %convert_element_type.204, () %tuple.121, (pred[256,256]{0,1:T(8,128)(4,1)}, bf16[256,256]{1,0:T(8,128)(2,1)}, bf16[256,2,4,128]{0,3,2,1:T(8,128)(2,1)}, f32[2,4,256]{2,1,0:T(4,128)}, ...), branch_computations={%region_13.13_spmd, %region_14.14_spmd} | conditional | flops 675282944 | bytes 16203828 | solution.py:189
  286.5 5.6 %conditional.6 = (f32[256,2,4,128]{3,0,2,1:T(8,128)S(1)}, f32[256,256]{0,1:T(8,128)S(1)}, f32[256,256]{0,1:T(8,128)S(1)}) conditional(s32[]{:T(128)} %convert_element_type.204, () %tuple.121, (pred[256,256]{0,1:T(8,128)(4,1)}, bf16[256,256]{1,0:T(8,128)(2,1)}, bf16[256,2,4,128]{0,3,2,1:T(8,128)(2,1)}, f32[2,4,256]{2,1,0:T(4,128)}, ...), branch_computations={%region_13.13_spmd, %region_14.14_spmd} | conditional | flops 675282944 | bytes 16203828 | solution.py:189
  311.9 5.6 %conditional.6 = (f32[256,2,4,128]{3,0,2,1:T(8,128)S(1)}, f32[256,256]{0,1:T(8,128)S(1)}, f32[256,256]{0,1:T(8,128)S(1)}) conditional(s32[]{:T(128)} %convert_element_type.204, () %tuple.121, (pred[256,256]{0,1:T(8,128)(4,1)}, bf16[256,256]{1,0:T(8,128)(2,1)}, bf16[256,2,4,128]{0,3,2,1:T(8,128)(2,1)}, f32[2,4,256]{2,1,0:T(4,128)}, ...), branch_computations={%region_13.13_spmd, %region_14.14_spmd} | conditional | flops 675282944 | bytes 16203828 | solution.py:189
  319.3 5.9 %collective-permute-done.3 = bf16[256,256]{0,1:T(8,128)(2,1)S(1)} collective-permute-done((bf16[256,256]{0,1:T(8,128)(2,1)S(1)}, bf16[256,256]{0,1:T(8,128)(2,1)S(1)}, u32[]{:S(2)}, u32[]{:S(2)}) %collective-permute-start.3) | collective-permute-done | bytes 131104 | tf_op jit(solution)/shard_map/while/body/eval_jaxpr/ppermute | solution.py:25
  339.6 5.6 %conditional.6 = (f32[256,2,4,128]{3,0,2,1:T(8,128)S(1)}, f32[256,256]{0,1:T(8,128)S(1)}, f32[256,256]{0,1:T(8,128)S(1)}) conditional(s32[]{:T(128)} %convert_element_type.204, () %tuple.121, (pred[256,256]{0,1:T(8,128)(4,1)}, bf16[256,256]{1,0:T(8,128)(2,1)}, bf16[256,2,4,128]{0,3,2,1:T(8,128)(2,1)}, f32[2,4,256]{2,1,0:T(4,128)}, ...), branch_computations={%region_13.13_spmd, %region_14.14_spmd} | conditional | flops 675282944 | bytes 16203828 | solution.py:189
  349.2 5.1 collective-permute-done.3
  364.7 5.6 %conditional.6 = (f32[256,2,4,128]{3,0,2,1:T(8,128)S(1)}, f32[256,256]{0,1:T(8,128)S(1)}, f32[256,256]{0,1:T(8,128)S(1)}) conditional(s32[]{:T(128)} %convert_element_type.204, () %tuple.121, (pred[256,256]{0,1:T(8,128)(4,1)}, bf16[256,256]{1,0:T(8,128)(2,1)}, bf16[256,2,4,128]{0,3,2,1:T(8,128)(2,1)}, f32[2,4,256]{2,1,0:T(4,128)}, ...), branch_computations={%region_13.13_spmd, %region_14.14_spmd} | conditional | flops 675282944 | bytes 16203828 | solution.py:189
  373.1 6.3 %collective-permute-done.3 = bf16[256,256]{0,1:T(8,128)(2,1)S(1)} collective-permute-done((bf16[256,256]{0,1:T(8,128)(2,1)S(1)}, bf16[256,256]{0,1:T(8,128)(2,1)S(1)}, u32[]{:S(2)}, u32[]{:S(2)}) %collective-permute-start.3) | collective-permute-done | bytes 131104 | tf_op jit(solution)/shard_map/while/body/eval_jaxpr/ppermute | solution.py:25
  389.4 5.6 %conditional.6 = (f32[256,2,4,128]{3,0,2,1:T(8,128)S(1)}, f32[256,256]{0,1:T(8,128)S(1)}, f32[256,256]{0,1:T(8,128)S(1)}) conditional(s32[]{:T(128)} %convert_element_type.204, () %tuple.121, (pred[256,256]{0,1:T(8,128)(4,1)}, bf16[256,256]{1,0:T(8,128)(2,1)}, bf16[256,2,4,128]{0,3,2,1:T(8,128)(2,1)}, f32[2,4,256]{2,1,0:T(4,128)}, ...), branch_computations={%region_13.13_spmd, %region_14.14_spmd} | conditional | flops 675282944 | bytes 16203828 | solution.py:189
  407.1 4.8 all-to-all-start.5
  414.1 6.1 %all-to-all-done.5 = bf16[8,64,256]{2,1,0:T(8,128)(2,1)S(1)} async-done(((bf16[8,64,256]{2,1,0:T(8,128)(2,1)}), bf16[8,64,256]{2,1,0:T(8,128)(2,1)S(1)}, u32[]{:S(2)}, u32[]{:S(2)}) %all-to-all-start.5) | async-done | bytes 262176 | tf_op jit(solution)/shard_map/all_to_all | solution.py:249
  426.6 10.0 %all-to-all-done.4 = bf16[8,64,256]{2,1,0:T(8,128)(2,1)S(1)} async-done(((bf16[8,64,256]{2,1,0:T(8,128)(2,1)}), bf16[8,64,256]{2,1,0:T(8,128)(2,1)S(1)}, u32[]{:S(2)}, u32[]{:S(2)}) %all-to-all-start.4) | async-done | bytes 262176 | tf_op jit(solution)/shard_map/all_to_all | solution.py:246
  440.9 15.6 %all-to-all-done.3 = bf16[8,64,1024]{2,1,0:T(8,128)(2,1)S(1)} async-done(((bf16[8,64,1024]{2,1,0:T(8,128)(2,1)}), bf16[8,64,1024]{2,1,0:T(8,128)(2,1)S(1)}, u32[]{:S(2)}, u32[]{:S(2)}) %all-to-all-start.3) | async-done | bytes 1048608 | tf_op jit(solution)/shard_map/all_to_all | solution.py:243
  457.5 19.1 %fusion.57 = f32[256,8192]{1,0:T(8,128)} fusion(bf16[256,1024]{1,0:T(8,128)(2,1)S(1)} %bitcast.128, bf16[8192,1024]{1,0:T(8,128)(2,1)} %param.16), kind=kOutput, calls=%fused_computation.93 | convolution fusion | flops 4294967296 | bytes 25690112 | tf_op jit(solution)/shard_map/dot_general | solution.py:53
  476.6 6.1 %convolution_add_fusion.1 = f32[256,8192]{1,0:T(8,128)S(1)} fusion(f32[256,8192]{1,0:T(8,128)} %fusion.57, bf16[256,256]{1,0:T(8,128)(2,1)S(1)} %bitcast.133, bf16[8192,256]{1,0:T(8,128)(2,1)} %param.17), kind=kOutput, calls=%fused_computation.39 | convolution fusion | flops 1075838976 | bytes 21102592 | tf_op jit(solution)/shard_map/dot_general | solution.py:53
  488.6 40.6 %reduce-scatter.2.cloned.1.call-done = bf16[256,2048]{1,0:T(8,128)(2,1)} async-done(((bf16[256,8192]{1,0:T(8,128)(2,1)}), bf16[256,2048]{1,0:T(8,128)(2,1)}) %reduce-scatter.2.cloned.1.call-update) | async-done | bytes 1048592 | tf_op jit(solution)/shard_map/reduce_scatter | solution.py:268
  (358 shorter events, 281.2 us)
Async XLA Ops:
  7.2 39.6 %all-gather.3.cloned.1.call-start = ((), (), s32[]{:S(2)}) async-start(), calls=%async_computation.7 | async-start | bytes 5242880 | tf_op jit(solution)/shard_map/all_gather | solution.py:72
  52.6 14.8 %all-to-all-start.1 = ((bf16[8,64,256]{2,1,0:T(8,128)(2,1)}), bf16[8,64,256]{2,1,0:T(8,128)(2,1)S(1)}, u32[]{:S(2)}, u32[]{:S(2)}) async-start(bf16[8,64,256]{2,1,0:T(8,128)(2,1)} %copy.107), calls=%async_computation.1 | async-start | bytes 524288 | tf_op jit(solution)/shard_map/all_to_all | solution.py:93
  67.4 12.5 %all-to-all-start = ((bf16[8,64,256]{2,1,0:T(8,128)(2,1)}), bf16[8,64,256]{2,1,0:T(8,128)(2,1)S(1)}, u32[]{:S(2)}, u32[]{:S(2)}) async-start(bf16[8,64,256]{2,1,0:T(8,128)(2,1)} %copy.103), calls=%async_computation | async-start | bytes 524288 | tf_op jit(solution)/shard_map/all_to_all | solution.py:90
  71.0 71.8 %all-gather.5.cloned.1.call-start = ((), (), s32[]{:S(2)}) async-start(), calls=%async_computation.8 | async-start | bytes 2359296 | tf_op jit(solution)/shard_map/all_gather | solution.py:14
  96.5 43.1 %all-to-all-start.2 = ((bf16[8,64,1024]{2,1,0:T(8,128)(2,1)}), bf16[8,64,1024]{2,1,0:T(8,128)(2,1)S(1)}, u32[]{:S(2)}, u32[]{:S(2)}) async-start(bf16[8,64,1024]{2,1,0:T(8,128)(2,1)} %copy.111), calls=%async_computation.2 | async-start | bytes 2097152 | tf_op jit(solution)/shard_map/all_to_all | solution.py:87
  205.0 24.4 %collective-permute-start = (bf16[256,256]{1,0:T(8,128)(2,1)}, bf16[256,256]{1,0:T(8,128)(2,1)}, u32[]{:S(2)}, u32[]{:S(2)}) collective-permute-start(bf16[256,256]{1,0:T(8,128)(2,1)} %copy.227), channel_id=1, source_target_pairs={{0,4},{4,8},{8,12},{12,16},{16,20},{20,24},{24,28},{28,0},{1,5},{5... | collective-permute-start | bytes 393224 | tf_op jit(solution)/shard_map/while/body/eval_jaxpr/ppermute | solution.py:25
  208.1 21.4 %collective-permute-start.1 = (bf16[256,256]{1,0:T(8,128)(2,1)}, bf16[256,256]{1,0:T(8,128)(2,1)}, u32[]{:S(2)}, u32[]{:S(2)}) collective-permute-start(bf16[256,256]{1,0:T(8,128)(2,1)} %copy.228), channel_id=1, source_target_pairs={{0,4},{4,8},{8,12},{12,16},{16,20},{20,24},{24,28},{28,0},{1,5},{5... | collective-permute-start | bytes 393224 | tf_op jit(solution)/shard_map/while/body/eval_jaxpr/ppermute | solution.py:25
  218.0 9.1 %collective-permute-start.3 = (bf16[256,256]{0,1:T(8,128)(2,1)S(1)}, bf16[256,256]{0,1:T(8,128)(2,1)S(1)}, u32[]{:S(2)}, u32[]{:S(2)}) collective-permute-start(bf16[256,256]{0,1:T(8,128)(2,1)S(1)} %fusion.86), channel_id=1, source_target_pairs={{0,4},{4,8},{8,12},{12,16},{16,20},{20,24},{24,28},{28,0},{1,5},{5... | collective-permute-start | bytes 393224 | tf_op jit(solution)/shard_map/while/body/eval_jaxpr/ppermute | solution.py:25
  231.0 22.1 %collective-permute-start = (bf16[256,256]{1,0:T(8,128)(2,1)}, bf16[256,256]{1,0:T(8,128)(2,1)}, u32[]{:S(2)}, u32[]{:S(2)}) collective-permute-start(bf16[256,256]{1,0:T(8,128)(2,1)} %copy.227), channel_id=1, source_target_pairs={{0,4},{4,8},{8,12},{12,16},{16,20},{20,24},{24,28},{28,0},{1,5},{5... | collective-permute-start | bytes 393224 | tf_op jit(solution)/shard_map/while/body/eval_jaxpr/ppermute | solution.py:25
  232.6 20.5 %collective-permute-start.1 = (bf16[256,256]{1,0:T(8,128)(2,1)}, bf16[256,256]{1,0:T(8,128)(2,1)}, u32[]{:S(2)}, u32[]{:S(2)}) collective-permute-start(bf16[256,256]{1,0:T(8,128)(2,1)} %copy.228), channel_id=1, source_target_pairs={{0,4},{4,8},{8,12},{12,16},{16,20},{20,24},{24,28},{28,0},{1,5},{5... | collective-permute-start | bytes 393224 | tf_op jit(solution)/shard_map/while/body/eval_jaxpr/ppermute | solution.py:25
  242.6 8.4 %collective-permute-start.3 = (bf16[256,256]{0,1:T(8,128)(2,1)S(1)}, bf16[256,256]{0,1:T(8,128)(2,1)S(1)}, u32[]{:S(2)}, u32[]{:S(2)}) collective-permute-start(bf16[256,256]{0,1:T(8,128)(2,1)S(1)} %fusion.86), channel_id=1, source_target_pairs={{0,4},{4,8},{8,12},{12,16},{16,20},{20,24},{24,28},{28,0},{1,5},{5... | collective-permute-start | bytes 393224 | tf_op jit(solution)/shard_map/while/body/eval_jaxpr/ppermute | solution.py:25
  254.7 24.4 %collective-permute-start = (bf16[256,256]{1,0:T(8,128)(2,1)}, bf16[256,256]{1,0:T(8,128)(2,1)}, u32[]{:S(2)}, u32[]{:S(2)}) collective-permute-start(bf16[256,256]{1,0:T(8,128)(2,1)} %copy.227), channel_id=1, source_target_pairs={{0,4},{4,8},{8,12},{12,16},{16,20},{20,24},{24,28},{28,0},{1,5},{5... | collective-permute-start | bytes 393224 | tf_op jit(solution)/shard_map/while/body/eval_jaxpr/ppermute | solution.py:25
  256.2 22.8 %collective-permute-start.1 = (bf16[256,256]{1,0:T(8,128)(2,1)}, bf16[256,256]{1,0:T(8,128)(2,1)}, u32[]{:S(2)}, u32[]{:S(2)}) collective-permute-start(bf16[256,256]{1,0:T(8,128)(2,1)} %copy.228), channel_id=1, source_target_pairs={{0,4},{4,8},{8,12},{12,16},{16,20},{20,24},{24,28},{28,0},{1,5},{5... | collective-permute-start | bytes 393224 | tf_op jit(solution)/shard_map/while/body/eval_jaxpr/ppermute | solution.py:25
  280.6 22.7 %collective-permute-start = (bf16[256,256]{1,0:T(8,128)(2,1)}, bf16[256,256]{1,0:T(8,128)(2,1)}, u32[]{:S(2)}, u32[]{:S(2)}) collective-permute-start(bf16[256,256]{1,0:T(8,128)(2,1)} %copy.227), channel_id=1, source_target_pairs={{0,4},{4,8},{8,12},{12,16},{16,20},{20,24},{24,28},{28,0},{1,5},{5... | collective-permute-start | bytes 393224 | tf_op jit(solution)/shard_map/while/body/eval_jaxpr/ppermute | solution.py:25
  282.2 21.2 %collective-permute-start.1 = (bf16[256,256]{1,0:T(8,128)(2,1)}, bf16[256,256]{1,0:T(8,128)(2,1)}, u32[]{:S(2)}, u32[]{:S(2)}) collective-permute-start(bf16[256,256]{1,0:T(8,128)(2,1)} %copy.228), channel_id=1, source_target_pairs={{0,4},{4,8},{8,12},{12,16},{16,20},{20,24},{24,28},{28,0},{1,5},{5... | collective-permute-start | bytes 393224 | tf_op jit(solution)/shard_map/while/body/eval_jaxpr/ppermute | solution.py:25
  304.9 22.4 %collective-permute-start = (bf16[256,256]{1,0:T(8,128)(2,1)}, bf16[256,256]{1,0:T(8,128)(2,1)}, u32[]{:S(2)}, u32[]{:S(2)}) collective-permute-start(bf16[256,256]{1,0:T(8,128)(2,1)} %copy.227), channel_id=1, source_target_pairs={{0,4},{4,8},{8,12},{12,16},{16,20},{20,24},{24,28},{28,0},{1,5},{5... | collective-permute-start | bytes 393224 | tf_op jit(solution)/shard_map/while/body/eval_jaxpr/ppermute | solution.py:25
  306.5 20.9 %collective-permute-start.1 = (bf16[256,256]{1,0:T(8,128)(2,1)}, bf16[256,256]{1,0:T(8,128)(2,1)}, u32[]{:S(2)}, u32[]{:S(2)}) collective-permute-start(bf16[256,256]{1,0:T(8,128)(2,1)} %copy.228), channel_id=1, source_target_pairs={{0,4},{4,8},{8,12},{12,16},{16,20},{20,24},{24,28},{28,0},{1,5},{5... | collective-permute-start | bytes 393224 | tf_op jit(solution)/shard_map/while/body/eval_jaxpr/ppermute | solution.py:25
  328.9 27.8 %collective-permute-start = (bf16[256,256]{1,0:T(8,128)(2,1)}, bf16[256,256]{1,0:T(8,128)(2,1)}, u32[]{:S(2)}, u32[]{:S(2)}) collective-permute-start(bf16[256,256]{1,0:T(8,128)(2,1)} %copy.227), channel_id=1, source_target_pairs={{0,4},{4,8},{8,12},{12,16},{16,20},{20,24},{24,28},{28,0},{1,5},{5... | collective-permute-start | bytes 393224 | tf_op jit(solution)/shard_map/while/body/eval_jaxpr/ppermute | solution.py:25
  332.0 24.7 %collective-permute-start.1 = (bf16[256,256]{1,0:T(8,128)(2,1)}, bf16[256,256]{1,0:T(8,128)(2,1)}, u32[]{:S(2)}, u32[]{:S(2)}) collective-permute-start(bf16[256,256]{1,0:T(8,128)(2,1)} %copy.228), channel_id=1, source_target_pairs={{0,4},{4,8},{8,12},{12,16},{16,20},{20,24},{24,28},{28,0},{1,5},{5... | collective-permute-start | bytes 393224 | tf_op jit(solution)/shard_map/while/body/eval_jaxpr/ppermute | solution.py:25
  345.3 9.1 %collective-permute-start.3 = (bf16[256,256]{0,1:T(8,128)(2,1)S(1)}, bf16[256,256]{0,1:T(8,128)(2,1)S(1)}, u32[]{:S(2)}, u32[]{:S(2)}) collective-permute-start(bf16[256,256]{0,1:T(8,128)(2,1)S(1)} %fusion.86), channel_id=1, source_target_pairs={{0,4},{4,8},{8,12},{12,16},{16,20},{20,24},{24,28},{28,0},{1,5},{5... | collective-permute-start | bytes 393224 | tf_op jit(solution)/shard_map/while/body/eval_jaxpr/ppermute | solution.py:25
  346.7 9.2 %collective-permute-start.2 = (bf16[256,256]{0,1:T(8,128)(2,1)S(1)}, bf16[256,256]{0,1:T(8,128)(2,1)S(1)}, u32[]{:S(2)}, u32[]{:S(2)}) collective-permute-start(bf16[256,256]{0,1:T(8,128)(2,1)S(1)} %fusion.85), channel_id=1, source_target_pairs={{0,4},{4,8},{8,12},{12,16},{16,20},{20,24},{24,28},{28,0},{1,5},{5... | collective-permute-start | bytes 393224 | tf_op jit(solution)/shard_map/while/body/eval_jaxpr/ppermute | solution.py:25
  358.3 23.8 %collective-permute-start = (bf16[256,256]{1,0:T(8,128)(2,1)}, bf16[256,256]{1,0:T(8,128)(2,1)}, u32[]{:S(2)}, u32[]{:S(2)}) collective-permute-start(bf16[256,256]{1,0:T(8,128)(2,1)} %copy.227), channel_id=1, source_target_pairs={{0,4},{4,8},{8,12},{12,16},{16,20},{20,24},{24,28},{28,0},{1,5},{5... | collective-permute-start | bytes 393224 | tf_op jit(solution)/shard_map/while/body/eval_jaxpr/ppermute | solution.py:25
  359.8 22.2 %collective-permute-start.1 = (bf16[256,256]{1,0:T(8,128)(2,1)}, bf16[256,256]{1,0:T(8,128)(2,1)}, u32[]{:S(2)}, u32[]{:S(2)}) collective-permute-start(bf16[256,256]{1,0:T(8,128)(2,1)} %copy.228), channel_id=1, source_target_pairs={{0,4},{4,8},{8,12},{12,16},{16,20},{20,24},{24,28},{28,0},{1,5},{5... | collective-permute-start | bytes 393224 | tf_op jit(solution)/shard_map/while/body/eval_jaxpr/ppermute | solution.py:25
  370.3 9.1 %collective-permute-start.3 = (bf16[256,256]{0,1:T(8,128)(2,1)S(1)}, bf16[256,256]{0,1:T(8,128)(2,1)S(1)}, u32[]{:S(2)}, u32[]{:S(2)}) collective-permute-start(bf16[256,256]{0,1:T(8,128)(2,1)S(1)} %fusion.86), channel_id=1, source_target_pairs={{0,4},{4,8},{8,12},{12,16},{16,20},{20,24},{24,28},{28,0},{1,5},{5... | collective-permute-start | bytes 393224 | tf_op jit(solution)/shard_map/while/body/eval_jaxpr/ppermute | solution.py:25
  371.4 9.9 %collective-permute-start.2 = (bf16[256,256]{0,1:T(8,128)(2,1)S(1)}, bf16[256,256]{0,1:T(8,128)(2,1)S(1)}, u32[]{:S(2)}, u32[]{:S(2)}) collective-permute-start(bf16[256,256]{0,1:T(8,128)(2,1)S(1)} %fusion.85), channel_id=1, source_target_pairs={{0,4},{4,8},{8,12},{12,16},{16,20},{20,24},{24,28},{28,0},{1,5},{5... | collective-permute-start | bytes 393224 | tf_op jit(solution)/shard_map/while/body/eval_jaxpr/ppermute | solution.py:25
  383.6 22.3 %collective-permute-start = (bf16[256,256]{1,0:T(8,128)(2,1)}, bf16[256,256]{1,0:T(8,128)(2,1)}, u32[]{:S(2)}, u32[]{:S(2)}) collective-permute-start(bf16[256,256]{1,0:T(8,128)(2,1)} %copy.227), channel_id=1, source_target_pairs={{0,4},{4,8},{8,12},{12,16},{16,20},{20,24},{24,28},{28,0},{1,5},{5... | collective-permute-start | bytes 393224 | tf_op jit(solution)/shard_map/while/body/eval_jaxpr/ppermute | solution.py:25
  385.2 20.8 %collective-permute-start.1 = (bf16[256,256]{1,0:T(8,128)(2,1)}, bf16[256,256]{1,0:T(8,128)(2,1)}, u32[]{:S(2)}, u32[]{:S(2)}) collective-permute-start(bf16[256,256]{1,0:T(8,128)(2,1)} %copy.228), channel_id=1, source_target_pairs={{0,4},{4,8},{8,12},{12,16},{16,20},{20,24},{24,28},{28,0},{1,5},{5... | collective-permute-start | bytes 393224 | tf_op jit(solution)/shard_map/while/body/eval_jaxpr/ppermute | solution.py:25
  396.1 9.1 %collective-permute-start.2 = (bf16[256,256]{0,1:T(8,128)(2,1)S(1)}, bf16[256,256]{0,1:T(8,128)(2,1)S(1)}, u32[]{:S(2)}, u32[]{:S(2)}) collective-permute-start(bf16[256,256]{0,1:T(8,128)(2,1)S(1)} %fusion.85), channel_id=1, source_target_pairs={{0,4},{4,8},{8,12},{12,16},{16,20},{20,24},{24,28},{28,0},{1,5},{5... | collective-permute-start | bytes 393224 | tf_op jit(solution)/shard_map/while/body/eval_jaxpr/ppermute | solution.py:25
  407.1 13.0 %all-to-all-start.5 = ((bf16[8,64,256]{2,1,0:T(8,128)(2,1)}), bf16[8,64,256]{2,1,0:T(8,128)(2,1)S(1)}, u32[]{:S(2)}, u32[]{:S(2)}) async-start(bf16[8,64,256]{2,1,0:T(8,128)(2,1)} %copy.132), calls=%async_computation.5 | async-start | bytes 524288 | tf_op jit(solution)/shard_map/all_to_all | solution.py:249
  420.1 16.5 %all-to-all-start.4 = ((bf16[8,64,256]{2,1,0:T(8,128)(2,1)}), bf16[8,64,256]{2,1,0:T(8,128)(2,1)S(1)}, u32[]{:S(2)}, u32[]{:S(2)}) async-start(bf16[8,64,256]{2,1,0:T(8,128)(2,1)} %copy.127), calls=%async_computation.4 | async-start | bytes 524288 | tf_op jit(solution)/shard_map/all_to_all | solution.py:246
  436.6 19.9 %all-to-all-start.3 = ((bf16[8,64,1024]{2,1,0:T(8,128)(2,1)}), bf16[8,64,1024]{2,1,0:T(8,128)(2,1)S(1)}, u32[]{:S(2)}, u32[]{:S(2)}) async-start(bf16[8,64,1024]{2,1,0:T(8,128)(2,1)} %copy.122), calls=%async_computation.3 | async-start | bytes 2097152 | tf_op jit(solution)/shard_map/all_to_all | solution.py:243
  440.2 89.0 %reduce-scatter.2.cloned.1.call-start = ((), (), s32[]{:S(2)}) async-start(), calls=%async_computation.9 | async-start | bytes 5242880 | tf_op jit(solution)/shard_map/reduce_scatter | solution.py:268
  (33 other events, 500.0 us)
Sparse Core Ops, SparseCore 0:
  9.6 37.1 all-gather.2
  82.7 60.0 all-gather.4
  486.1 42.9 reduce-scatter.1
